TPU v7x, 32 devices: a whole 2x2x4 slice. The times are simulated.
32 devices in a mesh: chan: 8 (over z, x), tm: 4 (over y, core).
Axes of the slice: x: 2, y: 2, z: 4, core: 2. Of those that a mesh axis runs over, the one named last changes fastest.
Arguments:
- samples: bfloat16 [2048, 131072], P('chan', 'tm'), may hold values from -6 to 6
- fir_taps: float32 [8, 4096], replicated, may hold values from -2 to 2
- beam_y: bfloat16 [2, 32, 32], replicated, may hold values from -0.75 to 0.75
- beam_x: bfloat16 [2, 64, 64], replicated, may hold values from -0.5 to 0.5
- delays: int32 [64, 2048], replicated, may hold values from 0 to 8, as said below
Outputs:
- series: float32 [2048, 32, 64], P('chan', 'tm')
Inputs may be any that keep to these rules, and one draw needn't show every extreme that they name: Each trial's delays come from a dispersion law: along a row they never rise with the channel index; the largest value is reached.
All inputs are finite; a program needn't handle non-finite values.
Results may differ from a plain program's by a relative error of at most 0.00068.
Values may be sent and summed in bfloat16 or wider, within the bound.
No kernel may reach another device: no remote copies, remote signals or barrier semaphores. Data moves between devices by JAX's collectives and lax.ppermute only.
A program may use at most 192 MiB of HBM per device.

v0:
```python
import math
import jax
import jax.numpy as jnp
from jax import lax
from jax.sharding import PartitionSpec as P


def shifted(array, axis, by):
    count = lax.axis_size(axis)
    pairs = [(i, i + by) for i in range(count) if 0 <= i + by < count]
    return lax.ppermute(array, axis, pairs)


def phase_table(rows_count, cols_count, period):
    row_index = jnp.arange(rows_count, dtype=jnp.int32)[:, None]
    col_index = jnp.arange(cols_count, dtype=jnp.int32)[None, :]
    angle = (row_index * col_index % period).astype(jnp.float32) * (2.0 * math.pi / period)
    return (jnp.cos(angle), jnp.sin(angle))


def transform(frames_rows, nfft):
    bits = nfft.bit_length() - 1
    first = 1 << bits // 2
    second = nfft // first
    rows_count = frames_rows.shape[0]
    shaped = frames_rows.reshape(rows_count, first, second)
    highest = lax.Precision.HIGHEST
    cos_one, sin_one = phase_table(first, first, first)
    section_real = jnp.einsum("rab,ak->rkb", shaped, cos_one, precision=highest)
    section_imag = -jnp.einsum("rab,ak->rkb", shaped, sin_one, precision=highest)
    cos_twist, sin_twist = phase_table(first, second, nfft)
    twist_real = section_real * cos_twist[None] + section_imag * sin_twist[None]
    twist_imag = section_imag * cos_twist[None] - section_real * sin_twist[None]
    cos_two, sin_two = phase_table(second, second // 2, second)
    out_real = jnp.einsum("rkb,bm->rmk", twist_real, cos_two, precision=highest) + jnp.einsum(
        "rkb,bm->rmk", twist_imag, sin_two, precision=highest
    )
    out_imag = jnp.einsum("rkb,bm->rmk", twist_imag, cos_two, precision=highest) - jnp.einsum(
        "rkb,bm->rmk", twist_real, sin_two, precision=highest
    )
    scale = 1.0 / math.sqrt(nfft)
    return (
        out_real.reshape(rows_count, nfft // 2) * scale,
        out_imag.reshape(rows_count, nfft // 2) * scale,
    )


def complex_product(weights, real_part, imag_part, form):
    w_real = weights[0]
    w_imag = weights[1]
    out_real = jnp.einsum(form, w_real, real_part, preferred_element_type=jnp.float32) - jnp.einsum(
        form, w_imag, imag_part, preferred_element_type=jnp.float32
    )
    out_imag = jnp.einsum(form, w_real, imag_part, preferred_element_type=jnp.float32) + jnp.einsum(
        form, w_imag, real_part, preferred_element_type=jnp.float32
    )
    return (out_real, out_imag)


def dedisperse(extended, delay_block, spec_dev, trials, scale):
    beam_count = extended.shape[2]

    def turn(shift_value, total):
        piece = lax.dynamic_slice_in_dim(extended, shift_value, spec_dev, 0)
        selector = (delay_block == shift_value).astype(jnp.bfloat16)
        return total + jnp.einsum(
            "scb,tc->bst", piece, selector, preferred_element_type=jnp.float32
        )

    summed = lax.fori_loop(
        0, spec_dev + 1, turn, jnp.zeros((beam_count, spec_dev, trials), jnp.float32)
    )
    return summed * scale


def on_device(samples, fir_taps, beam_y, beam_x, delays):
    dish_dev, total_points = samples.shape
    taps_count, nfft = fir_taps.shape
    spec_dev = total_points // nfft
    side_x = beam_x.shape[1]
    side_y = beam_y.shape[1]
    trials, channels = delays.shape
    frames = samples.reshape(dish_dev, spec_dev, nfft)
    history = shifted(frames[:, spec_dev - taps_count + 1 :, :], "tm", 1)
    extended_frames = jnp.concatenate([history, frames], axis=1)
    filtered = jnp.zeros((dish_dev, spec_dev, nfft), jnp.float32)
    for tap_index in range(taps_count):
        offset = taps_count - 1 - tap_index
        filtered = filtered + fir_taps[tap_index][None, None, :] * extended_frames[
            :, offset : offset + spec_dev, :
        ].astype(jnp.float32)
    frame_rows = filtered.reshape(dish_dev * spec_dev, nfft)
    volt_real, volt_imag = transform(frame_rows, nfft)
    volts = jnp.stack(
        [
            volt_real.reshape(dish_dev, spec_dev, nfft // 2),
            volt_imag.reshape(dish_dev, spec_dev, nfft // 2),
        ],
        axis=2,
    ).astype(jnp.bfloat16)
    gathered = lax.all_to_all(volts, "chan", split_axis=3, concat_axis=0, tiled=True)
    items = gathered.shape[1]
    chan_dev = gathered.shape[3]
    grid = gathered.reshape(side_x, side_y, items, 2, chan_dev)
    part_real, part_imag = complex_product(
        beam_y, grid[:, :, :, 0], grid[:, :, :, 1], "py,xync->ncxp"
    )
    part_real = part_real.astype(jnp.bfloat16)
    part_imag = part_imag.astype(jnp.bfloat16)
    form_real, form_imag = complex_product(beam_x, part_real, part_imag, "qx,ncxp->ncqp")
    power = (form_real * form_real + form_imag * form_imag).reshape(
        items, chan_dev, side_x * side_y
    )
    powers = (power - jnp.mean(power, axis=2, keepdims=True)).astype(jnp.bfloat16)
    scale = 1.0 / math.sqrt(channels)
    chan_dev = powers.shape[1]
    following = shifted(powers, "tm", -1)
    extended = jnp.concatenate([powers, following], axis=0)
    local_delays = lax.dynamic_slice_in_dim(delays, lax.axis_index("chan") * chan_dev, chan_dev, 1)
    return lax.psum_scatter(
        dedisperse(extended, local_delays, spec_dev, trials, scale),
        "chan",
        scatter_dimension=0,
        tiled=True,
    )


def solution(mesh):
    return jax.shard_map(
        on_device,
        mesh=mesh,
        in_specs=(P("chan", "tm"), P(), P(), P(), P()),
        out_specs=P("chan", "tm", None),
        check_vma=False,
    )
```

profile of v0, /device:TPU:0, one launch (start us, length us, event | category | flops | bytes accessed | tf_op | source)
XLA Modules:
  0.0 1550.4 jit_solution(6742614575479663688)
XLA Ops:
  6.5 22.5 %copy.72 = bf16[256,32768]{0,1:T(8,128)(2,1)} copy(bf16[256,32768]{1,0:T(8,128)(2,1)} %param.7) | data formatting | bytes 33554432 | tf_op args[0]
  42.1 19.4 %copy.73 = bf16[256,7,4096]{2,0,1:T(8,128)(2,1)} copy(bf16[256,7,4096]{0,2,1:T(8,128)(2,1)} %slice.88) | data formatting | bytes 29360128 | tf_op jit(solution)/shard_map/slice | solution.py:84
  69.3 16.7 %collective-permute-done = bf16[256,7,4096]{2,0,1:T(8,128)(2,1)} collective-permute-done((bf16[256,7,4096]{2,0,1:T(8,128)(2,1)}, bf16[256,7,4096]{2,0,1:T(8,128)(2,1)}, u32[]{:S(2)}, u32[]{:S(2)}) %collective-permute-start) | collective-permute-done | bytes 14680096 | tf_op jit(solution)/shard_map/ppermute | solution.py:11
  86.0 19.3 %copy.74 = bf16[256,7,4096]{0,2,1:T(8,128)(2,1)} copy(bf16[256,7,4096]{2,0,1:T(8,128)(2,1)} %collective-permute-done) | data formatting | bytes 29360128 | tf_op jit(solution)/shard_map/ppermute | solution.py:11
  105.4 53.0 %multiply_add_fusion = f32[256,8,4096]{0,2,1:T(8,128)} fusion(bf16[256,8,4096]{0,2,1:T(8,128)(2,1)} %bitcast.115, bf16[256,7,4096]{0,2,1:T(8,128)(2,1)} %copy.74, f32[4096]{0:T(1024)S(1)} %bitcast.124, f32[4096]{0:T(1024)S(1)} %bitcast.125, f32[4096]{0:T(1024)S(1)} %bitcast.119, f32[4096]{0:T(1024)S(1)} %bitcast.120, f32[4096]{0:T(1024)S(1)} %bitcast.121, ...), kind=kLoop, calls=%fused_computation.21 | loop fusion | flops 251658240 | bytes 65142784 | tf_op jit(solution)/shard_map/add | solution.py:89
  158.4 31.9 %copy.75 = f32[256,8,4096]{2,1,0:T(8,128)} copy(f32[256,8,4096]{0,2,1:T(8,128)} %multiply_add_fusion) | data formatting | bytes 67108864 | tf_op jit(solution)/shard_map/add | solution.py:89
  190.3 52.7 %reshape_reshape.3 = f32[2048,64,64]{2,1,0:T(8,128)} reshape(f32[256,8,4096]{2,1,0:T(8,128)} %copy.75) | data formatting | bytes 67108864 | tf_op jit(solution)/shard_map/reshape;reshape | solution.py:26
  243.0 50.9 %copy.76 = f32[2048,64,64]{0,1,2:T(8,128)} copy(f32[2048,64,64]{2,1,0:T(8,128)} %reshape_reshape.3) | data formatting | bytes 67108864 | tf_op jit(solution)/shard_map/reshape;reshape | solution.py:26
  293.9 37.2 %fusion.44 = f32[64,2048,64]{1,0,2:T(8,128)} fusion(f32[2048,64,64]{0,1,2:T(8,128)} %copy.76), kind=kOutput, calls=%fused_computation.71 | convolution fusion | flops 6442508288 | bytes 67108864 | tf_op jit(solution)/shard_map/rab,ak->rkb/dot_general | solution.py:30
  331.1 55.2 %add_bitcast_fusion = (f32[2048,64,64]{0,1,2:T(8,128)}, f32[2048,64,64]{0,1,2:T(8,128)}) fusion(f32[64,2048,64]{1,0,2:T(8,128)} %fusion.44, f32[64,64]{0,1:T(8,128)S(1)} %get-tuple-element.138, f32[64,64]{0,1:T(8,128)S(1)} %get-tuple-element.139, f32[2048,64,64]{0,1,2:T(8,128)} %copy.76), kind=kOutput, calls=%fused_computation.20 | convolution fusion | flops 6501228544 | bytes 134250496 | tf_op jit(solution)/shard_map/rab,ak->rkb/dot_general | solution.py:29
  386.3 45.7 %fusion.10 = f32[32,2048,64]{1,0,2:T(8,128)} fusion(f32[2048,64,64]{0,1,2:T(8,128)} %get-tuple-element.125), kind=kOutput, calls=%fused_computation.24 | convolution fusion | flops 3221254144 | bytes 50331648 | tf_op jit(solution)/shard_map/rkb,bm->rmk/dot_general | solution.py:35
  432.0 46.2 %fusion.8 = f32[32,2048,64]{1,0,2:T(8,128)} fusion(f32[2048,64,64]{0,1,2:T(8,128)} %get-tuple-element.125), kind=kOutput, calls=%fused_computation.22 | convolution fusion | flops 3221254144 | bytes 50331648 | tf_op jit(solution)/shard_map/rkb,bm->rmk/dot_general | solution.py:38
  478.2 49.5 %fusion.23 = bf16[2048,32,64]{0,1,2:T(8,128)(2,1)} fusion(f32[32,2048,64]{1,0,2:T(8,128)} %fusion.10, f32[2048,64,64]{0,1,2:T(8,128)} %get-tuple-element.124), kind=kOutput, calls=%fused_computation.46 | convolution fusion | flops 3233837056 | bytes 58720256 | tf_op jit(solution)/shard_map/rkb,bm->rmk/dot_general | solution.py:35
  527.7 29.2 %copy.80 = bf16[2048,32,64]{2,1,0:T(8,128)(2,1)} copy(bf16[2048,32,64]{0,1,2:T(8,128)(2,1)} %fusion.23) | data formatting | bytes 16777216 | tf_op jit(solution)/shard_map/mul | solution.py:43
  556.9 23.4 %mul.337 = bf16[256,8,1,2048]{3,1,0,2:T(8,128)(2,1)} reshape(bf16[2048,32,64]{2,1,0:T(8,128)(2,1)} %copy.80) | data formatting | bytes 16777216 | tf_op jit(solution)/shard_map/mul | solution.py:43
  580.4 48.1 %fusion.24 = bf16[2048,32,64]{0,1,2:T(8,128)(2,1)} fusion(f32[32,2048,64]{1,0,2:T(8,128)} %fusion.8, f32[2048,64,64]{0,1,2:T(8,128)} %get-tuple-element.124), kind=kOutput, calls=%fused_computation.47 | convolution fusion | flops 3233837056 | bytes 58720256 | tf_op jit(solution)/shard_map/rkb,bm->rmk/dot_general | solution.py:38
  628.5 29.4 %copy.83 = bf16[2048,32,64]{2,1,0:T(8,128)(2,1)} copy(bf16[2048,32,64]{0,1,2:T(8,128)(2,1)} %fusion.24) | data formatting | bytes 16777216 | tf_op jit(solution)/shard_map/mul | solution.py:44
  657.9 23.4 %mul.340 = bf16[256,8,1,2048]{3,1,0,2:T(8,128)(2,1)} reshape(bf16[2048,32,64]{2,1,0:T(8,128)(2,1)} %copy.83) | data formatting | bytes 16777216 | tf_op jit(solution)/shard_map/mul | solution.py:44
  681.3 13.7 pad_maximum_fusion.1
  695.1 25.6 %copy.84 = bf16[256,8,2,2048]{0,1,2,3:T(8,128)(2,1)} copy(bf16[256,8,2,2048]{3,1,0,2:T(8,128)(2,1)} %pad_maximum_fusion.1) | data formatting | bytes 33554432 | tf_op jit(solution)/shard_map/stack | solution.py:94
  720.6 324.9 %all_to_all.15 = bf16[256,8,2,2048]{0,1,2,3:T(8,128)(2,1)} all-to-all(bf16[256,8,2,2048]{0,1,2,3:T(8,128)(2,1)} %copy.84), channel_id=1, replica_groups=mesh['chan'=8,'tm'=4] {'chan'}, dimensions={3} | all-to-all | bytes 33554432 | tf_op jit(solution)/shard_map/all_to_all | solution.py:101
  1045.5 25.7 %copy.86 = bf16[8,256,8,2,256]{4,2,3,1,0:T(8,128)(2,1)} copy(bf16[8,256,8,2,256]{1,2,3,4,0:T(8,128)(2,1)} %bitcast.117) | data formatting | bytes 33554432 | tf_op jit(solution)/shard_map/all_to_all | solution.py:101
  1097.2 13.8 fusion.39
  1111.0 16.0 %fusion.27 = f32[8,256,32,64]{1,3,2,0:T(8,128)} fusion(bf16[8,256,64,32]{1,3,0,2:T(8,128)(2,1)} %fusion.39, bf16[2,64,64]{2,1,0:T(8,128)(2,1)S(1)} %copy-done.6), kind=kOutput, calls=%fused_computation.52 | convolution fusion | flops 536870912 | bytes 25182208 | tf_op jit(solution)/shard_map/qx,ncxp->ncqp/dot_general | solution.py:51
  1139.2 13.7 fusion.38
  1153.0 16.0 %fusion.31 = f32[8,256,32,64]{1,3,2,0:T(8,128)} fusion(bf16[8,256,64,32]{1,3,0,2:T(8,128)(2,1)} %fusion.38, bf16[2,64,64]{2,1,0:T(8,128)(2,1)S(1)} %copy-done.6), kind=kOutput, calls=%fused_computation.56 | convolution fusion | flops 536870912 | bytes 25182208 | tf_op jit(solution)/shard_map/qx,ncxp->ncqp/dot_general | solution.py:51
  1169.0 23.3 %fusion.119 = (f32[8,256]{1,0:T(8,128)S(1)}, f32[8,256,64,32]{1,2,3,0:T(8,128)}) fusion(f32[8,256,32,64]{1,3,2,0:T(8,128)} %fusion.29, bf16[8,256,64,32]{1,3,0,2:T(8,128)(2,1)S(1)} %copy-done.4, bf16[2,64,64]{2,1,0:T(8,128)(2,1)S(1)} %copy-done.6, f32[8,256,32,64]{1,3,2,0:T(8,128)} %fusion.31, f32[8,256,32,64]{1,3,2,0:T(8,128)} %fusion.27), kind=kOutput, calls=%fused_computation.146 | convolution fusion | flops 562034688 | bytes 75522048 | tf_op jit(solution)/shard_map/qx,ncxp->ncqp/dot_general | solution.py:54
  1192.3 15.2 copy.93
  1213.8 60.9 %collective-permute-done.1 = bf16[8,256,2048]{1,2,0:T(8,128)(2,1)} collective-permute-done((bf16[8,256,2048]{1,2,0:T(8,128)(2,1)}, bf16[8,256,2048]{1,2,0:T(8,128)(2,1)}, u32[]{:S(2)}, u32[]{:S(2)}) %collective-permute-start.1) | collective-permute-done | bytes 8388640 | tf_op jit(solution)/shard_map/ppermute | solution.py:11
  1274.6 13.7 pad_maximum_fusion.2
  1288.3 82.9 %while.14 = (s32[]{:T(128)}, f32[2048,8,64]{0,2,1:T(8,128)}, s32[64,256]{1,0:T(8,128)S(1)}, bf16[16,256,2048]{1,2,0:T(8,128)(2,1)}, s32[]{:T(128)}, /*index=5*/s32[]{:T(128)}) while((s32[]{:T(128)}, f32[2048,8,64]{0,2,1:T(8,128)}, s32[64,256]{1,0:T(8,128)S(1)}, bf16[16,256,2048]{1,2,0:T(8,128)(2,1)}, s32[]{:T(128)}, ...), condition=%wide.region_2.3_spmd.clone, body=%wide.region_1.2_spmd.clone.sunk | while | flops 538984448 | bytes 16843852 | solution.py:70
  1376.1 167.2 %reduce-scatter.2.cloned.1.call-done = f32[256,8,64]{0,2,1:T(8,128)} async-done(((f32[2048,8,64]{0,2,1:T(8,128)}), f32[256,8,64]{0,2,1:T(8,128)}) %reduce-scatter.2.cloned.1.call-update) | async-done | bytes 524304 | tf_op jit(solution)/shard_map/reduce_scatter | solution.py:120
  (41 shorter events, 153.1 us)
Async XLA Ops:
  6.5 1207.2 %copy-start = (s32[64,2048]{1,0:T(8,128)S(1)}, s32[64,2048]{1,0:T(8,128)}, u32[]{:S(2)}) copy-start(s32[64,2048]{1,0:T(8,128)} %param.11) | copy-start | bytes 1572868
  6.5 1536.8 %reduce-scatter.2.cloned.1.call-start = ((), (), s32[]{:S(2)}) async-start(), calls=%async_computation.2 | async-start | bytes 4718592 | tf_op jit(solution)/shard_map/reduce_scatter | solution.py:120
  42.1 27.1 %copy-start.5 = (f32[8,4096]{1,0:T(8,128)S(1)}, f32[8,4096]{1,0:T(8,128)}, u32[]{:S(2)}) copy-start(f32[8,4096]{1,0:T(8,128)} %param.8) | copy-start | bytes 393220
  61.5 24.5 %collective-permute-start = (bf16[256,7,4096]{2,0,1:T(8,128)(2,1)}, bf16[256,7,4096]{2,0,1:T(8,128)(2,1)}, u32[]{:S(2)}, u32[]{:S(2)}) collective-permute-start(bf16[256,7,4096]{2,0,1:T(8,128)(2,1)} %copy.73), channel_id=1, source_target_pairs={{0,1},{1,2},{2,3},{4,5},{5,6},{6,7},{8,9},{9,10},{10,11},{12,13},{... | collective-permute-start | bytes 44040200 | tf_op jit(solution)/shard_map/ppermute | solution.py:11
  1071.3 9.8 copy-start.7
  1077.9 3.2 copy-start.2
  1077.9 11.3 copy-start.1
  1097.2 13.8 copy-start.6
  1111.0 16.0 %copy-start.3 = (bf16[8,256,64,32]{1,3,0,2:T(8,128)(2,1)S(1)}, bf16[8,256,64,32]{1,3,0,2:T(8,128)(2,1)}, u32[]{:S(2)}) copy-start(bf16[8,256,64,32]{1,3,0,2:T(8,128)(2,1)} %fusion.39) | copy-start | bytes 25165828
  1153.0 16.0 %copy-start.4 = (bf16[8,256,64,32]{1,3,0,2:T(8,128)(2,1)S(1)}, bf16[8,256,64,32]{1,3,0,2:T(8,128)(2,1)}, u32[]{:S(2)}) copy-start(bf16[8,256,64,32]{1,3,0,2:T(8,128)(2,1)} %fusion.38) | copy-start | bytes 25165828
  1212.4 62.2 %collective-permute-start.1 = (bf16[8,256,2048]{1,2,0:T(8,128)(2,1)}, bf16[8,256,2048]{1,2,0:T(8,128)(2,1)}, u32[]{:S(2)}, u32[]{:S(2)}) collective-permute-start(bf16[8,256,2048]{1,2,0:T(8,128)(2,1)} %fusion.22), channel_id=1, source_target_pairs={{1,0},{2,1},{3,2},{5,4},{6,5},{7,6},{9,8},{10,9},{11,10},{13,12},{... | collective-permute-start | bytes 25165832 | tf_op jit(solution)/shard_map/ppermute | solution.py:11
Sparse Core Ops, SparseCore 0:
  1376.2 166.9 reduce-scatter.1
where the time goes:
time: 1560 us; the launch traced here: 1550 us
  matrix products  476 us (31%)
  local copies, waits for them, and re-layouts  392 us (25%)
  blocking collectives  325 us (21%)
  waiting for transfers between devices  245 us (16%)
  other arithmetic  90.4 us (6%)
    all_to_all x1, blocking collectives, on_device(): lax.all_to_all(volts, 'chan', split_axis=3, concat_axis=0, tiled=True)  325 us
    reduce_scatter x1, waiting for transfers between devices, on_device(): lax.psum_scatter(dedisperse(extended, local_delays, spec_dev, trials, sca...  167 us
    another operation x2, local copies, waits for them, and re-layouts, transform(): shaped = frames_rows.reshape(rows_count, first, second)  104 us
    dot_general x9, matrix products, turn(): jnp.einsum('scb,tc->bst', piece, selector, preferred_element_type=jnp.flo...  82.9 us
    ppermute x2, waiting for transfers between devices, shifted(): return lax.ppermute(array, axis, pairs)  77.6 us
    dot_general x1, matrix products, transform(): section_real = jnp.einsum('rab,ak->rkb', shaped, cos_one, precision=highest)  55.2 us
    add x1, other arithmetic, on_device(): filtered + fir_taps[tap_index][None, None, :] * extended_frames[:, offset...  53 us
    mul x2, local copies, waits for them, and re-layouts, transform(): out_imag.reshape(rows_count, nfft // 2) * scale  52.9 us
  transfers between devices with their start and end apart: 3, of which 3 were waited for; matrix products, arithmetic and copies ran while one was open for 0% of the time, Pallas kernels for 0%

commit v1 on v0

--- a/solution.py
+++ b/solution.py
@@ -3,6 +3,17 @@
 import jax.numpy as jnp
 from jax import lax
 from jax.sharding import PartitionSpec as P
+
+
+def split_up(array, dim, devices):
+    before, after = (array.shape[:dim], array.shape[dim + 1 :])
+    return jnp.moveaxis(array.reshape(*before, devices, -1, *after), dim, 0)
+
+
+def laid_out(pieces, dim):
+    shape = list(pieces.shape[1:])
+    shape[dim] *= pieces.shape[0]
+    return jnp.moveaxis(pieces, 0, dim).reshape(shape)
 
 
 def shifted(array, axis, by):
@@ -98,7 +109,14 @@
         ],
         axis=2,
     ).astype(jnp.bfloat16)
-    gathered = lax.all_to_all(volts, "chan", split_axis=3, concat_axis=0, tiled=True)
+    length, index = (lax.axis_size("chan"), lax.axis_index("chan"))
+    parts = split_up(volts, 3, length)
+    finished = [parts[index]]
+    for step in range(1, length):
+        sent = parts[index ^ step]
+        finished.append(lax.ppermute(sent, "chan", [(i_2, i_2 ^ step) for i_2 in range(length)]))
+    parts = jnp.stack(finished)[index ^ jnp.arange(length)]
+    gathered = laid_out(parts, 0)
     items = gathered.shape[1]
     chan_dev = gathered.shape[3]
     grid = gathered.reshape(side_x, side_y, items, 2, chan_dev)

time: 1560 us -> 1630 us (1.045)
  blocking collectives: 325 us -> 0 us
  waiting for transfers between devices: 245 us -> 543 us
  local copies, waits for them, and re-layouts: 392 us -> 471 us
    all_to_all x1 -> x0, blocking collectives: 325 us -> none  [on_device(): lax.all_to_all(volts, 'chan', split_axis=3, concat_axis=0, tiled=True)]
    ppermute x2, waiting for transfers between devices: 77.6 us -> 210 us  [shifted(): return lax.ppermute(array, axis, pairs)]
    ppermute x0 -> x7, waiting for transfers between devices: none -> 123 us  [on_device(): lax.ppermute(sent, 'chan', [(i_2, i_2 ^ step) for i_2 in range(length)])]
    another operation x0 -> x9, local copies, waits for them, and re-layouts: none -> 83.5 us
    reduce_scatter x1, waiting for transfers between devices: 167 us -> 211 us  [on_device(): lax.psum_scatter(dedisperse(extended, local_delays, spec_dev, trials, sca...]
    all_to_all x1 -> x0, local copies, waits for them, and re-layouts: 25.7 us -> none  [on_device(): lax.all_to_all(volts, 'chan', split_axis=3, concat_axis=0, tiled=True)]
    gather x0 -> x3, local copies, waits for them, and re-layouts: none -> 22.2 us  [on_device(): parts = jnp.stack(finished)[index ^ jnp.arange(length)]]
    unnamed x17 -> x35, local copies, waits for them, and re-layouts: 25.7 us -> 43.6 us
  transfers between devices with their start and end apart: 3 -> 10, of which waited for: 3 -> 7; matrix products, arithmetic and copies ran while one was open for 0% -> 1% of each run, Pallas kernels for 0% -> 0%
where the time goes in v1:
time: 1630 us; the launch traced here: 1620 us
  waiting for transfers between devices  543 us (33%)
  matrix products  476 us (29%)
  local copies, waits for them, and re-layouts  471 us (29%)
  other arithmetic  90.5 us (6%)
  starting transfers between devices  22.8 us (1%)
    reduce_scatter x1, waiting for transfers between devices, on_device(): lax.psum_scatter(dedisperse(extended, local_delays, spec_dev, trials, sca...  211 us
    ppermute x2, waiting for transfers between devices, shifted(): return lax.ppermute(array, axis, pairs)  210 us
    ppermute x7, waiting for transfers between devices, on_device(): lax.ppermute(sent, 'chan', [(i_2, i_2 ^ step) for i_2 in range(length)])  123 us
    another operation x2, local copies, waits for them, and re-layouts, transform(): shaped = frames_rows.reshape(rows_count, first, second)  103 us
    another operation x8, local copies, waits for them, and re-layouts  83.3 us
    dot_general x9, matrix products, turn(): jnp.einsum('scb,tc->bst', piece, selector, preferred_element_type=jnp.flo...  82.9 us
    dot_general x1, matrix products, transform(): section_real = jnp.einsum('rab,ak->rkb', shaped, cos_one, precision=highest)  54.9 us
    add x1, other arithmetic, on_device(): filtered + fir_taps[tap_index][None, None, :] * extended_frames[:, offset...  53 us
  transfers between devices with their start and end apart: 10, of which 7 were waited for; matrix products, arithmetic and copies ran while one was open for 1% of the time, Pallas kernels for 0%

profile of v1, /device:TPU:0, one launch (start us, length us, event | category | flops | bytes accessed | tf_op | source)
XLA Modules:
  0.0 1616.8 jit_solution(15391788637939578460)
XLA Ops:
  6.5 22.5 %copy.63 = bf16[256,32768]{0,1:T(8,128)(2,1)} copy(bf16[256,32768]{1,0:T(8,128)(2,1)} %param.7) | data formatting | bytes 33554432 | tf_op args[0]
  42.1 19.3 %copy.64 = bf16[256,7,4096]{2,0,1:T(8,128)(2,1)} copy(bf16[256,7,4096]{0,2,1:T(8,128)(2,1)} %slice.92) | data formatting | bytes 29360128 | tf_op jit(solution)/shard_map/slice | solution.py:95
  69.3 16.7 %collective-permute-done = bf16[256,7,4096]{2,0,1:T(8,128)(2,1)} collective-permute-done((bf16[256,7,4096]{2,0,1:T(8,128)(2,1)}, bf16[256,7,4096]{2,0,1:T(8,128)(2,1)}, u32[]{:S(2)}, u32[]{:S(2)}) %collective-permute-start) | collective-permute-done | bytes 14680096 | tf_op jit(solution)/shard_map/ppermute | solution.py:22
  86.0 19.3 %copy.65 = bf16[256,7,4096]{0,2,1:T(8,128)(2,1)} copy(bf16[256,7,4096]{2,0,1:T(8,128)(2,1)} %collective-permute-done) | data formatting | bytes 29360128 | tf_op jit(solution)/shard_map/ppermute | solution.py:22
  105.3 53.0 %multiply_add_fusion = f32[256,8,4096]{0,2,1:T(8,128)} fusion(bf16[256,8,4096]{0,2,1:T(8,128)(2,1)} %bitcast.151, bf16[256,7,4096]{0,2,1:T(8,128)(2,1)} %copy.65, f32[4096]{0:T(1024)S(1)} %bitcast.166, f32[4096]{0:T(1024)S(1)} %bitcast.167, f32[4096]{0:T(1024)S(1)} %bitcast.161, f32[4096]{0:T(1024)S(1)} %bitcast.162, f32[4096]{0:T(1024)S(1)} %bitcast.163, ...), kind=kLoop, calls=%fused_computation.23 | loop fusion | flops 251658240 | bytes 65142784 | tf_op jit(solution)/shard_map/add | solution.py:100
  158.3 32.0 %copy.66 = f32[256,8,4096]{2,1,0:T(8,128)} copy(f32[256,8,4096]{0,2,1:T(8,128)} %multiply_add_fusion) | data formatting | bytes 67108864 | tf_op jit(solution)/shard_map/add | solution.py:100
  190.3 52.6 %reshape_reshape.6 = f32[2048,64,64]{2,1,0:T(8,128)} reshape(f32[256,8,4096]{2,1,0:T(8,128)} %copy.66) | data formatting | bytes 67108864 | tf_op jit(solution)/shard_map/reshape;reshape | solution.py:37
  242.9 50.8 %copy.67 = f32[2048,64,64]{0,1,2:T(8,128)} copy(f32[2048,64,64]{2,1,0:T(8,128)} %reshape_reshape.6) | data formatting | bytes 67108864 | tf_op jit(solution)/shard_map/reshape;reshape | solution.py:37
  293.8 37.0 %fusion.44 = f32[64,2048,64]{1,0,2:T(8,128)} fusion(f32[2048,64,64]{0,1,2:T(8,128)} %copy.67), kind=kOutput, calls=%fused_computation.88 | convolution fusion | flops 6442508288 | bytes 67108864 | tf_op jit(solution)/shard_map/rab,ak->rkb/dot_general | solution.py:41
  330.8 54.9 %add_bitcast_fusion = (f32[2048,64,64]{0,1,2:T(8,128)}, f32[2048,64,64]{0,1,2:T(8,128)}) fusion(f32[64,2048,64]{1,0,2:T(8,128)} %fusion.44, f32[64,64]{0,1:T(8,128)S(1)} %get-tuple-element.144, f32[64,64]{0,1:T(8,128)S(1)} %get-tuple-element.145, f32[2048,64,64]{0,1,2:T(8,128)} %copy.67), kind=kOutput, calls=%fused_computation.22 | convolution fusion | flops 6501228544 | bytes 134250496 | tf_op jit(solution)/shard_map/rab,ak->rkb/dot_general | solution.py:40
  385.6 46.2 %fusion.8 = f32[32,2048,64]{1,0,2:T(8,128)} fusion(f32[2048,64,64]{0,1,2:T(8,128)} %get-tuple-element.121), kind=kOutput, calls=%fused_computation.24 | convolution fusion | flops 3221254144 | bytes 50331648 | tf_op jit(solution)/shard_map/rkb,bm->rmk/dot_general | solution.py:49
  431.8 46.0 %fusion.10 = f32[32,2048,64]{1,0,2:T(8,128)} fusion(f32[2048,64,64]{0,1,2:T(8,128)} %get-tuple-element.121), kind=kOutput, calls=%fused_computation.26 | convolution fusion | flops 3221254144 | bytes 50331648 | tf_op jit(solution)/shard_map/rkb,bm->rmk/dot_general | solution.py:46
  477.8 48.3 %fusion.24 = bf16[2048,32,64]{0,1,2:T(8,128)(2,1)} fusion(f32[32,2048,64]{1,0,2:T(8,128)} %fusion.8, f32[2048,64,64]{0,1,2:T(8,128)} %get-tuple-element.120), kind=kOutput, calls=%fused_computation.49 | convolution fusion | flops 3233837056 | bytes 58720256 | tf_op jit(solution)/shard_map/rkb,bm->rmk/dot_general | solution.py:49
  526.1 29.1 %copy.74 = bf16[2048,32,64]{2,1,0:T(8,128)(2,1)} copy(bf16[2048,32,64]{0,1,2:T(8,128)(2,1)} %fusion.24) | data formatting | bytes 16777216 | tf_op jit(solution)/shard_map/mul | solution.py:55
  555.1 22.8 %mul.342 = bf16[256,8,1,8,256]{4,3,1,0,2:T(8,128)(2,1)} reshape(bf16[2048,32,64]{2,1,0:T(8,128)(2,1)} %copy.74) | data formatting | bytes 16777216 | tf_op jit(solution)/shard_map/mul | solution.py:55
  577.9 49.5 %fusion.23 = bf16[2048,32,64]{0,1,2:T(8,128)(2,1)} fusion(f32[32,2048,64]{1,0,2:T(8,128)} %fusion.10, f32[2048,64,64]{0,1,2:T(8,128)} %get-tuple-element.120), kind=kOutput, calls=%fused_computation.48 | convolution fusion | flops 3233837056 | bytes 58720256 | tf_op jit(solution)/shard_map/rkb,bm->rmk/dot_general | solution.py:46
  627.4 29.2 %copy.71 = bf16[2048,32,64]{2,1,0:T(8,128)(2,1)} copy(bf16[2048,32,64]{0,1,2:T(8,128)(2,1)} %fusion.23) | data formatting | bytes 16777216 | tf_op jit(solution)/shard_map/mul | solution.py:54
  656.6 22.8 %mul.339 = bf16[256,8,1,8,256]{4,3,1,0,2:T(8,128)(2,1)} reshape(bf16[2048,32,64]{2,1,0:T(8,128)(2,1)} %copy.71) | data formatting | bytes 16777216 | tf_op jit(solution)/shard_map/mul | solution.py:54
  695.9 74.0 %constant_dynamic-slice_fusion = (bf16[256,8,2,1,256]{4,3,1,0,2:T(2,128)(2,1)S(1)}, bf16[256,8,2,1,256]{4,3,1,0,2:T(2,128)(2,1)}, bf16[256,8,2,1,256]{4,3,1,0,2:...) fusion(bf16[256,8,2,8,256]{4,3,1,0,2:T(8,128)(2,1)} %constant_d, ...), kind=kLoop, calls=%fused_computation.145 | loop fusion | bytes 33554464 | tf_op jit(solution)/shard_map/dynamic-slice.7
  803.7 41.4 %collective-permute-done.2 = bf16[256,8,2,256]{3,1,2,0:T(8,128)(2,1)S(1)} collective-permute-done((bf16[256,8,2,256]{3,1,2,0:T(8,128)(2,1)S(1)}, bf16[256,8,2,256]{3,1,2,0:T(8,128)(2,1)S(1)}, u32[]{:S(2)}, u32[]{:S(2)}) %collective-permute-start.2) | collective-permute-done | bytes 2097184 | tf_op jit(solution)/shard_map/ppermute | solution.py:117
  850.4 16.8 %collective-permute-done.3 = bf16[256,8,2,256]{3,1,2,0:T(8,128)(2,1)} collective-permute-done((bf16[256,8,2,256]{3,1,2,0:T(8,128)(2,1)S(1)}, bf16[256,8,2,256]{3,1,2,0:T(8,128)(2,1)}, u32[]{:S(2)}, u32[]{:S(2)}) %collective-permute-start.3) | collective-permute-done | bytes 2097184 | tf_op jit(solution)/shard_map/ppermute | solution.py:117
  870.7 52.8 %collective-permute-done.5 = bf16[256,8,2,256]{3,1,2,0:T(8,128)(2,1)} collective-permute-done((bf16[256,8,2,256]{3,1,2,0:T(8,128)(2,1)S(1)}, bf16[256,8,2,256]{3,1,2,0:T(8,128)(2,1)}, u32[]{:S(2)}, u32[]{:S(2)}) %collective-permute-start.5) | collective-permute-done | bytes 2097184 | tf_op jit(solution)/shard_map/ppermute | solution.py:117
  987.9 13.8 fusion.39
  1001.7 16.0 fusion.27
  1030.0 13.7 fusion.38
  1043.7 16.0 fusion.31
  1059.7 23.4 %fusion.121 = (f32[8,256]{1,0:T(8,128)S(1)}, f32[8,256,64,32]{1,2,3,0:T(8,128)}) fusion(f32[8,256,32,64]{1,3,2,0:T(8,128)} %fusion.29, bf16[8,256,64,32]{1,3,0,2:T(8,128)(2,1)S(1)} %copy-done.4, bf16[2,64,64]{2,1,0:T(8,128)(2,1)S(1)} %copy-done.11, f32[8,256,32,64]{1,3,2,0:T(8,128)} %fusion.31, f32[8,256,32,64]{1,3,2,0:T(8,128)} %fusion.27), kind=kOutput, calls=%fused_computation.177 | convolution fusion | flops 562034688 | bytes 75522048 | tf_op jit(solution)/shard_map/qx,ncxp->ncqp/dot_general | solution.py:65
  1083.0 15.2 copy.89
  1104.5 193.1 %collective-permute-done.8 = bf16[8,256,2048]{1,2,0:T(8,128)(2,1)} collective-permute-done((bf16[8,256,2048]{1,2,0:T(8,128)(2,1)}, bf16[8,256,2048]{1,2,0:T(8,128)(2,1)}, u32[]{:S(2)}, u32[]{:S(2)}) %collective-permute-start.8) | collective-permute-done | bytes 8388640 | tf_op jit(solution)/shard_map/ppermute | solution.py:22
  1297.6 13.7 pad_maximum_fusion.2
  1311.3 82.9 %while.14 = (s32[]{:T(128)}, f32[2048,8,64]{0,2,1:T(8,128)}, s32[64,256]{1,0:T(8,128)S(1)}, bf16[16,256,2048]{1,2,0:T(8,128)(2,1)}, s32[]{:T(128)}, /*index=5*/s32[]{:T(128)}) while((s32[]{:T(128)}, f32[2048,8,64]{0,2,1:T(8,128)}, s32[64,256]{1,0:T(8,128)S(1)}, bf16[16,256,2048]{1,2,0:T(8,128)(2,1)}, s32[]{:T(128)}, ...), condition=%wide.region_2.3_spmd.clone, body=%wide.region_1.2_spmd.clone.sunk | while | flops 538984448 | bytes 16843852 | solution.py:81
  1399.2 210.5 %reduce-scatter.2.cloned.1.call-done = f32[256,8,64]{0,2,1:T(8,128)} async-done(((f32[2048,8,64]{0,2,1:T(8,128)}), f32[256,8,64]{0,2,1:T(8,128)}) %reduce-scatter.2.cloned.1.call-update) | async-done | bytes 524304 | tf_op jit(solution)/shard_map/reduce_scatter | solution.py:138
  (85 shorter events, 250.5 us)
Async XLA Ops:
  6.5 1097.9 %copy-start = (s32[64,2048]{1,0:T(8,128)S(1)}, s32[64,2048]{1,0:T(8,128)}, u32[]{:S(2)}) copy-start(s32[64,2048]{1,0:T(8,128)} %param.11) | copy-start | bytes 1572868
  6.5 1603.2 %reduce-scatter.2.cloned.1.call-start = ((), (), s32[]{:S(2)}) async-start(), calls=%async_computation.1 | async-start | bytes 4718592 | tf_op jit(solution)/shard_map/reduce_scatter | solution.py:138
  42.1 27.0 %copy-start.10 = (f32[8,4096]{1,0:T(8,128)S(1)}, f32[8,4096]{1,0:T(8,128)}, u32[]{:S(2)}) copy-start(f32[8,4096]{1,0:T(8,128)} %param.8) | copy-start | bytes 393220
  61.5 24.5 %collective-permute-start = (bf16[256,7,4096]{2,0,1:T(8,128)(2,1)}, bf16[256,7,4096]{2,0,1:T(8,128)(2,1)}, u32[]{:S(2)}, u32[]{:S(2)}) collective-permute-start(bf16[256,7,4096]{2,0,1:T(8,128)(2,1)} %copy.64), channel_id=1, source_target_pairs={{0,1},{1,2},{2,3},{4,5},{5,6},{6,7},{8,9},{9,10},{10,11},{12,13},{... | collective-permute-start | bytes 44040200 | tf_op jit(solution)/shard_map/ppermute | solution.py:22
  770.0 12.7 copy-start.7
  770.0 16.2 copy-start.6
  770.0 17.3 %copy-start.5 = (bf16[256,8,2,1,256]{4,3,1,0,2:T(2,128)(2,1)S(1)}, bf16[256,8,2,1,256]{4,3,1,0,2:T(2,128)(2,1)}, u32[]{:S(2)}) copy-start(bf16[256,8,2,1,256]{4,3,1,0,2:T(2,128)(2,1)} %get-tuple-element.127) | copy-start | bytes 6291460
  772.7 26.4 %collective-permute-start.1 = (bf16[256,8,2,256]{3,1,2,0:T(8,128)(2,1)S(1)}, bf16[256,8,2,256]{3,1,2,0:T(8,128)(2,1)S(1)}, u32[]{:S(2)}, u32[]{:S(2)}) collective-permute-start(bf16[256,8,2,256]{3,1,2,0:T(8,128)(2,1)S(1)} %bitcast.159), channel_id=1, source_target_pairs={{0,4},{4,0},{8,12},{12,8},{16,20},{20,16},{24,28},{28,24},{1,5},{5... | collective-permute-start | bytes 6291464 | tf_op jit(solution)/shard_map/ppermute | solution.py:117
  777.6 67.5 %collective-permute-start.2 = (bf16[256,8,2,256]{3,1,2,0:T(8,128)(2,1)S(1)}, bf16[256,8,2,256]{3,1,2,0:T(8,128)(2,1)S(1)}, u32[]{:S(2)}, u32[]{:S(2)}) collective-permute-start(bf16[256,8,2,256]{3,1,2,0:T(8,128)(2,1)S(1)} %bitcast.158), channel_id=1, source_target_pairs={{0,8},{4,12},{8,0},{12,4},{16,24},{20,28},{24,16},{28,20},{1,9},{5... | collective-permute-start | bytes 6291464 | tf_op jit(solution)/shard_map/ppermute | solution.py:117
  782.4 84.8 %collective-permute-start.3 = (bf16[256,8,2,256]{3,1,2,0:T(8,128)(2,1)S(1)}, bf16[256,8,2,256]{3,1,2,0:T(8,128)(2,1)}, u32[]{:S(2)}, u32[]{:S(2)}) collective-permute-start(bf16[256,8,2,256]{3,1,2,0:T(8,128)(2,1)S(1)} %bitcast.156), channel_id=1, source_target_pairs={{0,12},{4,8},{8,4},{12,0},{16,28},{20,24},{24,20},{28,16},{1,13},{... | collective-permute-start | bytes 6291464 | tf_op jit(solution)/shard_map/ppermute | solution.py:117
  783.0 86.0 %collective-permute-start.4 = (bf16[256,8,2,256]{3,1,2,0:T(8,128)(2,1)S(1)}, bf16[256,8,2,256]{3,1,2,0:T(8,128)(2,1)}, u32[]{:S(2)}, u32[]{:S(2)}) collective-permute-start(bf16[256,8,2,256]{3,1,2,0:T(8,128)(2,1)S(1)} %bitcast.155), channel_id=1, source_target_pairs={{0,16},{4,20},{8,24},{12,28},{16,0},{20,4},{24,8},{28,12},{1,17},{... | collective-permute-start | bytes 6291464 | tf_op jit(solution)/shard_map/ppermute | solution.py:117
  786.5 137.0 %collective-permute-start.5 = (bf16[256,8,2,256]{3,1,2,0:T(8,128)(2,1)S(1)}, bf16[256,8,2,256]{3,1,2,0:T(8,128)(2,1)}, u32[]{:S(2)}, u32[]{:S(2)}) collective-permute-start(bf16[256,8,2,256]{3,1,2,0:T(8,128)(2,1)S(1)} %bitcast.154), channel_id=1, source_target_pairs={{0,20},{4,16},{8,28},{12,24},{16,4},{20,0},{24,12},{28,8},{1,21},{... | collective-permute-start | bytes 6291464 | tf_op jit(solution)/shard_map/ppermute | solution.py:117
  799.1 47.0 %copy-start.8 = (bf16[256,8,2,256]{3,1,2,0:T(8,128)(2,1)}, bf16[256,8,2,256]{3,1,2,0:T(8,128)(2,1)S(1)}, u32[]{:S(2)}) copy-start(bf16[256,8,2,256]{3,1,2,0:T(8,128)(2,1)S(1)} %collective-permute-done.1) | copy-start | bytes 6291460
  799.1 126.2 %collective-permute-start.6 = (bf16[256,8,2,256]{3,1,2,0:T(8,128)(2,1)S(1)}, bf16[256,8,2,256]{3,1,2,0:T(8,128)(2,1)S(1)}, u32[]{:S(2)}, u32[]{:S(2)}) collective-permute-start(bf16[256,8,2,256]{3,1,2,0:T(8,128)(2,1)S(1)} %bitcast.153), channel_id=1, source_target_pairs={{0,24},{4,28},{8,16},{12,20},{16,8},{20,12},{24,0},{28,4},{1,25},{... | collective-permute-start | bytes 6291464 | tf_op jit(solution)/shard_map/ppermute | solution.py:117
  845.1 1.4 copy-start.9
  845.1 80.3 %collective-permute-start.7 = (bf16[256,8,2,256]{3,1,2,0:T(8,128)(2,1)S(1)}, bf16[256,8,2,256]{3,1,2,0:T(8,128)(2,1)S(1)}, u32[]{:S(2)}, u32[]{:S(2)}) collective-permute-start(bf16[256,8,2,256]{3,1,2,0:T(8,128)(2,1)S(1)} %bitcast.157), channel_id=1, source_target_pairs={{0,28},{4,24},{8,20},{12,16},{16,12},{20,8},{24,4},{28,0},{1,29},{... | collective-permute-start | bytes 6291464 | tf_op jit(solution)/shard_map/ppermute | solution.py:117
  961.5 10.3 copy-start.12
  968.5 3.2 copy-start.2
  968.6 11.3 copy-start.1
  987.9 13.8 copy-start.11
  1001.7 16.0 copy-start.3
  1043.7 16.0 copy-start.4
  1103.2 194.4 %collective-permute-start.8 = (bf16[8,256,2048]{1,2,0:T(8,128)(2,1)}, bf16[8,256,2048]{1,2,0:T(8,128)(2,1)}, u32[]{:S(2)}, u32[]{:S(2)}) collective-permute-start(bf16[8,256,2048]{1,2,0:T(8,128)(2,1)} %fusion.22), channel_id=1, source_target_pairs={{1,0},{2,1},{3,2},{5,4},{6,5},{7,6},{9,8},{10,9},{11,10},{13,12},{... | collective-permute-start | bytes 25165832 | tf_op jit(solution)/shard_map/ppermute | solution.py:22
Sparse Core Ops, SparseCore 0:
  1399.3 210.3 reduce-scatter.1
